TPU v7x, 128 devices: a whole 4x4x4 slice. The times are simulated.
128 devices in a mesh: expert: 32 (over z, x, core), replica: 4 (over y).
Axes of the slice: x: 4, y: 4, z: 4, core: 2. Of those that a mesh axis runs over, the one named last changes fastest.
Arguments:
- atom_rows: bfloat16 [16384, 512], P(('expert', 'replica')), may hold values from -6 to 6
- grad_out: bfloat16 [16384, 512], P(('expert', 'replica')), may hold values from -6 to 6
- expert_ids: int32 [16384, 1], P(('expert', 'replica')), may hold values from 0 to 31; in each aligned block of 128 rows (0 to 127, 128 to 255, ...) at most 8 rows name the same one
- weight_in: bfloat16 [32, 512, 4096], P('expert', None, 'replica'), may hold values from -0.25 to 0.25
- weight_out: bfloat16 [32, 4096, 512], P('expert', 'replica'), may hold values from -0.09375 to 0.09375
Outputs:
- grad_atoms: bfloat16 [16384, 512], P(('expert', 'replica'))
- grad_weight_in: float32 [32, 512, 4096], P('expert', None, 'replica')
- grad_weight_out: float32 [32, 4096, 512], P('expert', 'replica')
Inputs may be any that keep to these rules, and one draw needn't show every extreme that they name: `expert_ids`: in each aligned block of 128 rows (the rows of one device) no expert is named by more than 8 rows, and in some block one expert is named by exactly 8 rows; every expert is named somewhere.
All inputs are finite; a program needn't handle non-finite values.
Results may differ from a plain program's by a relative error of at most 0.0049.
Values may be sent and summed in bfloat16 or wider, within the bound.
No kernel may reach another device: no remote copies, remote signals or barrier semaphores. Data moves between devices by JAX's collectives and lax.ppermute only.
A program may use at most 64 MiB of HBM per device.

v0:
```python
import functools

import jax
import jax.numpy as jnp
from jax import lax
from jax.experimental import pallas as pl
from jax.experimental.pallas import tpu as pltpu
from jax.sharding import PartitionSpec as P


VMEM = pl.BlockSpec(memory_space=pltpu.VMEM)
SMEM = pl.BlockSpec(memory_space=pltpu.SMEM)
HBM = pl.BlockSpec(memory_space=pltpu.HBM)
DMA = pltpu.SemaphoreType.DMA
BF16 = jnp.bfloat16
F32 = jnp.float32


def limit(mib):
    return pltpu.CompilerParams(vmem_limit_bytes=mib << 20)


def slots_of(labels, experts, capacity):
    rows = labels.shape[1]
    named = lax.broadcasted_iota(jnp.int32, (experts, rows), 0) == labels
    earlier = lax.broadcasted_iota(jnp.int32, (rows, rows), 0) < lax.broadcasted_iota(jnp.int32, (rows, rows), 1)
    before = jnp.dot(named.astype(F32).astype(BF16), earlier.astype(F32).astype(BF16), preferred_element_type=F32)
    place = jnp.sum(jnp.where(named, before, 0.0), axis=0, keepdims=True)
    return labels * capacity + place.astype(jnp.int32)


def slot_table(slots, count):
    table = lax.broadcasted_iota(jnp.int32, (count, slots.shape[1]), 0) == slots
    return table.astype(F32).astype(BF16)


def pack_kernel(experts, capacity, ids_hbm, rows_hbm, grad_hbm, out, slots, ids, rows, grad, sems):
    copies = [
        pltpu.make_async_copy(src, dst, sems.at[i])
        for i, (src, dst) in enumerate(((ids_hbm, ids), (rows_hbm, rows), (grad_hbm, grad)))
    ]
    for copy in copies:
        copy.start()
    copies[0].wait()
    slots[...] = slots_of(ids[...], experts, capacity)
    table = slot_table(slots[...], experts * capacity)
    width = rows.shape[1]
    for i, ref in enumerate((rows, grad)):
        copies[1 + i].wait()
        out[:, pl.ds(i * width, width)] = jnp.dot(table, ref[...], preferred_element_type=F32).astype(BF16)


def pack(ids, rows, grad, experts, capacity):
    shape = (experts * capacity, 2 * rows.shape[1])
    ids, rows, grad = (pltpu.with_memory_space_constraint(x, pltpu.HBM) for x in (ids, rows, grad))
    return pl.pallas_call(
        functools.partial(pack_kernel, experts, capacity),
        out_shape=(jax.ShapeDtypeStruct(shape, BF16), jax.ShapeDtypeStruct(ids.shape, ids.dtype)),
        in_specs=[HBM] * 3,
        out_specs=(VMEM, VMEM),
        scratch_shapes=[
            pltpu.VMEM(ids.shape, ids.dtype),
            pltpu.VMEM(rows.shape, rows.dtype),
            pltpu.VMEM(grad.shape, grad.dtype),
            DMA((3,)),
        ],
        compiler_params=limit(4),
        name="pack",
    )(ids, rows, grad)


def unpack_kernel(experts, replicas, capacity, slots_ref, parts_ref, out_ref):
    table = slot_table(slots_ref[...], experts * capacity)
    total = parts_ref[:, 0].astype(F32)
    for replica in range(1, replicas):
        total = total + parts_ref[:, replica].astype(F32)
    total = total.astype(BF16).reshape(experts * capacity, out_ref.shape[1])
    out_ref[...] = lax.dot_general(
        table, total, (((0,), (0,)), ((), ())), preferred_element_type=F32
    ).astype(BF16)


def unpack(slots, parts, experts, replicas, capacity):
    return pl.pallas_call(
        functools.partial(unpack_kernel, experts, replicas, capacity),
        out_shape=jax.ShapeDtypeStruct((slots.shape[1], parts.shape[-1]), BF16),
        in_specs=[VMEM] * 2,
        out_specs=VMEM,
        compiler_params=limit(8),
        name="unpack",
    )(slots, parts)


def group_math(pieces, win_ref, wout_ref, keep):
    width = win_ref.shape[0]
    hidden = win_ref.shape[1]
    tile = 256
    both = jnp.concatenate([piece[...] for piece in pieces], axis=0)
    rows_in, rows_grad = both[:, :width], both[:, width:]
    total = None
    for at in range(0, hidden, tile):
        win = win_ref[:, at : at + tile]
        preact = jnp.dot(rows_in, win, preferred_element_type=F32)
        grad_act = lax.dot_general(
            rows_grad, wout_ref[at : at + tile, :], (((1,), (1,)), ((), ())), preferred_element_type=F32
        )
        gate_sig = jax.nn.sigmoid(preact)
        grad_pre = (grad_act * gate_sig * (1.0 + preact * (1.0 - gate_sig))).astype(BF16)
        if keep is not None:
            keep(at, tile, (preact * gate_sig).astype(BF16), grad_pre)
        part = lax.dot_general(grad_pre, win, (((1,), (1,)), ((), ())), preferred_element_type=F32)
        total = part if total is None else total + part
    return total.astype(BF16)


def keep_rows(pieces, rows_hbm, sems):
    copies = []
    at = 0
    for piece in pieces:
        rows = pl.ds(at, piece.shape[0])
        at += piece.shape[0]
        copies.append(pltpu.make_async_copy(piece, rows_hbm.at[rows], sems.at[len(copies)]))
        copies[-1].start()
    return copies


def group_kernel(count, *refs):
    win_ref, wout_ref, act_hbm, pre_hbm, rows_hbm, part_ref, act_ref, pre_ref, sems, rows_sems = refs[count:]
    copies = keep_rows(refs[:count], rows_hbm, rows_sems)
    others = len(copies)

    def keep(at, tile, *values):
        columns = pl.ds(at, tile)
        for value, ref, hbm in zip(values, (act_ref, pre_ref), (act_hbm, pre_hbm)):
            ref[:, columns] = value
            copies.append(pltpu.make_async_copy(ref.at[:, columns], hbm.at[:, columns], sems.at[len(copies) - others]))
            copies[-1].start()

    part_ref[...] = group_math(refs[:count], win_ref, wout_ref, keep).reshape(part_ref.shape)
    for copy in copies:
        copy.wait()


def last_kernel(count, where_ref, *refs):
    win_ref, wout_ref, own_ref, near_ref, late_ref, out_hbm, rows_hbm, part, sems, rows_sems = refs[count:]
    sources, replicas = out_hbm.shape[:2]
    cut = sources // 2
    at = [lax.rem(where_ref[0] + k, replicas) for k in range(replicas)]
    copies = []

    def put(ref, low, high):
        for first, replica in ((0, low), (cut, high)):
            rows = pl.ds(first, cut)
            copies.append(pltpu.make_async_copy(ref.at[rows], out_hbm.at[rows, replica], sems.at[len(copies)]))
            copies[-1].start()

    put(own_ref, at[0], at[0])
    put(near_ref, at[3], at[1])
    put(late_ref, at[1], at[3])
    kept = keep_rows(refs[:count], rows_hbm, rows_sems)
    part[...] = group_math(refs[:count], win_ref, wout_ref, None).reshape(part.shape)
    put(part, at[2], at[2])
    for copy in copies + kept:
        copy.wait()


def cost(rows, width, hidden):
    return pl.CostEstimate(
        flops=6 * rows * width * hidden, bytes_accessed=4 * width * hidden, transcendentals=rows * hidden
    )


def group(pieces, win, wout, capacity):
    rows = sum(piece.shape[0] for piece in pieces)
    width, hidden = win.shape
    return pl.pallas_call(
        functools.partial(group_kernel, len(pieces)),
        out_shape=(
            pltpu.HBM((rows, hidden), BF16),
            pltpu.HBM((rows, hidden), BF16),
            pltpu.HBM((rows, 2 * width), BF16),
            jax.ShapeDtypeStruct((rows // capacity, capacity, width), BF16),
        ),
        in_specs=[VMEM] * (len(pieces) + 2),
        out_specs=(HBM, HBM, HBM, VMEM),
        scratch_shapes=[
            pltpu.VMEM((rows, hidden), BF16),
            pltpu.VMEM((rows, hidden), BF16),
            DMA((8,)),
            DMA((len(pieces),)),
        ],
        compiler_params=limit(16),
        cost_estimate=cost(rows, width, hidden),
        name="group",
    )(*pieces, win, wout)


def last_group(where, pieces, win, wout, own, near, late, replicas):
    rows = sum(piece.shape[0] for piece in pieces)
    width, hidden = win.shape
    sources, capacity = own.shape[:2]
    return pl.pallas_call(
        functools.partial(last_kernel, len(pieces)),
        out_shape=(
            pltpu.HBM((sources, replicas, capacity, width), BF16),
            pltpu.HBM((rows, 2 * width), BF16),
        ),
        in_specs=[SMEM] + [VMEM] * (len(pieces) + 5),
        out_specs=(HBM, HBM),
        scratch_shapes=[pltpu.VMEM(own.shape, BF16), DMA((8,)), DMA((len(pieces),))],
        compiler_params=limit(16),
        cost_estimate=cost(rows, width, hidden),
        name="last_group",
    )(where, *pieces, win, wout, own, near, late)


def again_kernel(rows_ref, win_ref, wout_ref, act_ref, pre_ref):
    width = win_ref.shape[0]
    rows = rows_ref[...]
    preact = jnp.dot(rows[:, :width], win_ref[...], preferred_element_type=F32)
    grad_act = lax.dot_general(rows[:, width:], wout_ref[...], (((1,), (1,)), ((), ())), preferred_element_type=F32)
    gate_sig = jax.nn.sigmoid(preact)
    act_ref[...] = (preact * gate_sig).astype(BF16)
    pre_ref[...] = (grad_act * gate_sig * (1.0 + preact * (1.0 - gate_sig))).astype(BF16)


def again(rows, win, wout):
    width, hidden = win.shape
    tile = 256
    out = jax.ShapeDtypeStruct((rows.shape[0], hidden), BF16)
    return pl.pallas_call(
        again_kernel,
        out_shape=(out, out),
        grid=(hidden // tile,),
        in_specs=[
            VMEM,
            pl.BlockSpec((width, tile), lambda j: (0, j)),
            pl.BlockSpec((tile, width), lambda j: (j, 0)),
        ],
        out_specs=(pl.BlockSpec((rows.shape[0], tile), lambda j: (0, j)),) * 2,
        cost_estimate=pl.CostEstimate(
            flops=4 * rows.shape[0] * width * hidden,
            bytes_accessed=4 * width * hidden,
            transcendentals=rows.shape[0] * hidden,
        ),
        name="again",
    )(rows, win, wout)


def weights_kernel(pieces, groups, *refs):
    rows_refs, act_refs, pre_refs = refs[:pieces], refs[pieces : pieces + groups], refs[pieces + groups : pieces + 2 * groups]
    first_ref, second_ref, turned = refs[pieces + 2 * groups :]
    width, _ = first_ref.shape

    @pl.when(pl.program_id(0) == 0)
    def _():
        rows = jnp.concatenate([ref[:, :width] for ref in rows_refs], axis=0)
        turned[...] = rows.T

    pre = jnp.concatenate([ref[...] for ref in pre_refs], axis=0)
    first_ref[...] = jnp.dot(turned[...], pre, preferred_element_type=F32)
    act = jnp.concatenate([ref[...] for ref in act_refs], axis=0)
    grad = jnp.concatenate([ref[:, width:] for ref in rows_refs], axis=0)
    second_ref[...] = lax.dot_general(act, grad, (((0,), (0,)), ((), ())), preferred_element_type=F32)


def weight_grads(pieces, acts, pres, width):
    rows = sum(piece.shape[0] for piece in pieces)
    hidden = acts[0].shape[1]
    tile = 256
    return pl.pallas_call(
        functools.partial(weights_kernel, len(pieces), len(acts)),
        out_shape=(
            jax.ShapeDtypeStruct((width, hidden), F32),
            jax.ShapeDtypeStruct((hidden, width), F32),
        ),
        grid=(hidden // tile,),
        in_specs=[VMEM] * len(pieces) + [pl.BlockSpec((act.shape[0], tile), lambda j: (0, j)) for act in acts + pres],
        out_specs=(pl.BlockSpec((width, tile), lambda j: (0, j)), pl.BlockSpec((tile, width), lambda j: (j, 0))),
        scratch_shapes=[pltpu.VMEM((width, rows), BF16)],
        cost_estimate=pl.CostEstimate(
            flops=4 * rows * width * hidden, bytes_accessed=8 * width * hidden, transcendentals=0
        ),
        name="weights",
    )(*pieces, *acts, *pres)


def steps(atom_rows, grad_out, expert_ids, weight_in, weight_out):
    experts = lax.axis_size("expert")
    replicas = lax.axis_size("replica")
    local_rows = atom_rows.shape[0]
    width = atom_rows.shape[1]
    capacity = 2 * local_rows // experts
    win, wout = weight_in[0], weight_out[0]
    ids = expert_ids.reshape(1, local_rows)
    where = lax.axis_index("replica").astype(jnp.int32).reshape(1)
    packed, slots = pack(ids, atom_rows, grad_out, experts, capacity)
    own = lax.all_to_all(
        packed.reshape(experts, capacity, 2 * width), "expert", split_axis=0, concat_axis=0, tiled=True
    ).reshape(experts * capacity, 2 * width)
    up = [(i, (i + 1) % replicas) for i in range(replicas)]
    down = [(i, (i - 1) % replicas) for i in range(replicas)]
    half = experts * capacity // 2
    low, high = own[:half], own[half:]

    def send(rows, way):
        return lax.ppermute(rows, "replica", way)

    below_low = send(low, up)
    above_high = send(high, down)
    below_high = send(high, up)
    above_low = send(low, down)
    far_low = send(below_low, up)
    far_high = send(above_high, down)
    act0, pre0, rows0, part0 = group([low, high], win, wout, capacity)
    act1, pre1, rows1, part1 = group([below_low, above_high], win, wout, capacity)
    act2, pre2, rows2, part2 = group([above_low, below_high], win, wout, capacity)
    sending, rows3 = last_group(where, [far_low, far_high], win, wout, part0, part1, part2, replicas)
    returned = lax.all_to_all(
        sending.reshape(experts * replicas, capacity, width),
        ("expert", "replica"),
        split_axis=0,
        concat_axis=0,
        tiled=True,
    )
    act3, pre3 = again(rows3, weight_in[0], weight_out[0])
    grad_first, grad_second = weight_grads(
        [rows0, rows1, rows2, rows3],
        [act0, act1, act2, act3],
        [pre0, pre1, pre2, pre3],
        width,
    )
    grad_rows = unpack(slots, returned.reshape(experts, replicas, capacity, width), experts, replicas, capacity)
    return (grad_rows, grad_first[None], grad_second[None])


def solution(mesh):
    rows = P(("expert", "replica"), None)
    first = P("expert", None, "replica")
    second = P("expert", "replica", None)
    return jax.shard_map(
        steps,
        mesh=mesh,
        in_specs=(rows, rows, rows, first, second),
        out_specs=(rows, first, second),
        check_vma=False,
    )
```

profile of v0, /device:TPU:1, one launch (start us, length us, event | category | flops | bytes accessed | tf_op | source)
XLA Modules:
  0.0 73.0 jit_solution(12482340705762306838)
XLA Ops:
  0.6 0.0 copy-start.1
  0.6 0.0 copy-start
  0.7 1.5 %pack.1 = (bf16[256,1024]{1,0:T(8,128)(2,1)S(1)}, s32[1,128]{1,0:T(1,128)S(1)}) custom-call(s32[1,128]{1,0:T(1,128)} %bitcast.26, bf16[128,512]{1,0:T(8,128)(2,1)} %rows_hbm.1, bf16[128,512]{1,0:T(8,128)(2,1)} %grad_hbm.1), custom_call_target="tpu_custom_call" | custom-call | tf_op jit(solution)/shard_map/pack/pallas_call | solution.py:56
  2.2 20.7 %all_to_all.10 = bf16[32,8,1024]{2,1,0:T(8,128)(2,1)S(1)} all-to-all(bf16[32,8,1024]{2,1,0:T(8,128)(2,1)S(1)} %bitcast.24), channel_id=1, replica_groups=mesh['expert'=32,'replica'=4] {'expert'}, dimensions={0} | all-to-all | bytes 1048576 | tf_op jit(solution)/shard_map/all_to_all | solution.py:298
  22.9 2.8 %collective-permute-start.2 = (bf16[128,1024]{1,0:T(8,128)(2,1)S(1)}, bf16[128,1024]{1,0:T(8,128)(2,1)S(1)}, u32[]{:S(2)}, u32[]{:S(2)}) collective-permute-start(bf16[128,1024]{1,0:T(8,128)(2,1)S(1)} %get-tuple-element.43.refs_1_), channel_id=1, source_target_pairs={{0,3},{1,0},{2,1},{3,2},{4,7},{5,4},{6,5},{7,6},{8,11},{9,8},{10,9... | collective-permute-start | bytes 786440 | tf_op jit(solution)/shard_map/ppermute | solution.py:307
  25.7 0.0 collective-permute-start
  25.7 0.0 collective-permute-start.5
  25.7 2.7 %collective-permute-start.4 = (bf16[128,1024]{1,0:T(8,128)(2,1)S(1)}, bf16[128,1024]{1,0:T(8,128)(2,1)}, u32[]{:S(2)}, u32[]{:S(2)}) collective-permute-start(bf16[128,1024]{1,0:T(8,128)(2,1)S(1)} %get-tuple-element.44.refs_0_), channel_id=1, source_target_pairs={{0,3},{1,0},{2,1},{3,2},{4,7},{5,4},{6,5},{7,6},{8,11},{9,8},{10,9... | collective-permute-start | bytes 786440 | tf_op jit(solution)/shard_map/ppermute | solution.py:307
  28.4 2.6 %collective-permute-done.2.refs_1_ = bf16[128,1024]{1,0:T(8,128)(2,1)S(1)} collective-permute-done((bf16[128,1024]{1,0:T(8,128)(2,1)S(1)}, bf16[128,1024]{1,0:T(8,128)(2,1)S(1)}, u32[]{:S(2)}, u32[]{:S(2)}) %collective-permute-start.2) | collective-permute-done | bytes 262176 | tf_op jit(solution)/shard_map/ppermute | solution.py:307
  30.9 3.4 %collective-permute-start.3 = (bf16[128,1024]{1,0:T(8,128)(2,1)S(1)}, bf16[128,1024]{1,0:T(8,128)(2,1)S(1)}, u32[]{:S(2)}, u32[]{:S(2)}) collective-permute-start(bf16[128,1024]{1,0:T(8,128)(2,1)S(1)} %collective-permute-done.2.refs_1_), channel_id=1, source_target_pairs={{0,3},{1,0},{2,1},{3,2},{4,7},{5,4},{6,5},{7,6},{8,11},{9,8},{10,9... | collective-permute-start | bytes 786440 | tf_op jit(solution)/shard_map/ppermute | solution.py:307
  34.4 0.0 collective-permute-done.refs_0_
  34.4 0.0 collective-permute-start.1
  34.4 0.0 copy-done.1
  34.4 0.0 copy-done
  34.4 2.1 %group.3 = (bf16[256,1024]{1,0:T(8,128)(2,1)}, bf16[256,1024]{1,0:T(8,128)(2,1)}, bf16[256,1024]{1,0:T(8,128)(2,1)}, bf16[32,8,512]{2,1,0:T(8,128)(2,1)S(1)}) custom-call(bf16[128,1024]{1,0:T(8,128)(2,1)S(1)} %get-tuple-element.44.refs_0_, bf16[128,1024]{1,0:T(8,128)(2,1)S(1)} %get-tuple-element.43.refs_1_, bf16[512,1024]{1,0:T(8,128)(2,1)S(1)} %bitcast.14, ...), custom_call_target="tpu_custom_call" | custom-call | flops 805306368 | bytes 2097152 | tf_op jit(solution)/shard_map/group/pallas_call | solution.py:176
  36.5 3.0 %group.4 = (bf16[256,1024]{1,0:T(8,128)(2,1)}, bf16[256,1024]{1,0:T(8,128)(2,1)}, bf16[256,1024]{1,0:T(8,128)(2,1)}, bf16[32,8,512]{2,1,0:T(8,128)(2,1)S(1)}) custom-call(bf16[128,1024]{1,0:T(8,128)(2,1)} %collective-permute-done.refs_0_, bf16[128,1024]{1,0:T(8,128)(2,1)S(1)} %collective-permute-done.2.refs_1_, bf16[512,1024]{1,0:T(8,128)(2,1)S(1)} %bitcast.15, ...), custom_call_target="tpu_custom_call" | custom-call | flops 805306368 | bytes 2097152 | tf_op jit(solution)/shard_map/group/pallas_call | solution.py:176
  39.5 0.3 collective-permute-done.5.refs_1_
  39.8 0.0 collective-permute-done.4.refs_0_
  39.8 3.1 %group.5 = (bf16[256,1024]{1,0:T(8,128)(2,1)}, bf16[256,1024]{1,0:T(8,128)(2,1)}, bf16[256,1024]{1,0:T(8,128)(2,1)}, bf16[32,8,512]{2,1,0:T(8,128)(2,1)S(1)}) custom-call(bf16[128,1024]{1,0:T(8,128)(2,1)} %collective-permute-done.4.refs_0_, bf16[128,1024]{1,0:T(8,128)(2,1)} %collective-permute-done.5.refs_1_, bf16[512,1024]{1,0:T(8,128)(2,1)S(1)} %bitcast.16, ...), custom_call_target="tpu_custom_call" | custom-call | flops 805306368 | bytes 2097152 | tf_op jit(solution)/shard_map/group/pallas_call | solution.py:176
  42.9 0.0 collective-permute-done.3.refs_1_
  42.9 2.4 %collective-permute-done.1.refs_0_ = bf16[128,1024]{1,0:T(8,128)(2,1)S(1)} collective-permute-done((bf16[128,1024]{1,0:T(8,128)(2,1)}, bf16[128,1024]{1,0:T(8,128)(2,1)S(1)}, u32[]{:S(2)}, u32[]{:S(2)}) %collective-permute-start.1) | collective-permute-done | bytes 262176 | tf_op jit(solution)/shard_map/ppermute | solution.py:307
  45.3 2.2 %last_group.1 = (bf16[32,4,8,512]{3,2,1,0:T(8,128)(2,1)}, bf16[256,1024]{1,0:T(8,128)(2,1)}) custom-call(s32[1]{0:T(128)} %bitcast.1.where_ref, bf16[128,1024]{1,0:T(8,128)(2,1)S(1)} %collective-permute-done.1.refs_0_, bf16[128,1024]{1,0:T(8,128)(2,1)S(1)} %collective-permute-done.3.refs_1_, bf16[512,1024]{1,0:T(8,128)(2,1)S(1)} %bitcast.17, ...), custom_call_target="tpu_custom_call" | custom-call | flops 805306368 | bytes 2097152 | tf_op jit(solution)/shard_map/last_group/pallas_call | solution.py:202
  47.5 5.3 %all-to-all-start.1 = ((bf16[128,8,512]{2,1,0:T(8,128)(2,1)}), bf16[128,8,512]{2,1,0:T(8,128)(2,1)S(1)}, u32[]{:S(2)}, u32[]{:S(2)}) async-start(bf16[128,8,512]{2,1,0:T(8,128)(2,1)} %bitcast.25), calls=%async_computation.1 | async-start | bytes 2097152 | tf_op jit(solution)/shard_map/all_to_all | solution.py:319
  52.8 4.4 %again.1 = (bf16[256,1024]{1,0:T(8,128)(2,1)}, bf16[256,1024]{1,0:T(8,128)(2,1)}) custom-call(bf16[256,1024]{1,0:T(8,128)(2,1)} %get-tuple-element.32.rows_ref.refs_3_, bf16[512,1024]{1,0:T(8,128)(2,1)} %bitcast.13, bf16[1024,512]{1,0:T(8,128)(2,1)} %bitcast.18), custom_call_target="tpu_custom_call" | custom-call | flops 536870912 | bytes 2097152 | tf_op jit(solution)/shard_map/again/pallas_call | solution.py:231
  57.2 7.4 %weights.1 = (f32[512,1024]{1,0:T(8,128)}, f32[1024,512]{1,0:T(8,128)}) custom-call(bf16[256,1024]{1,0:T(8,128)(2,1)} %get-tuple-element.29.refs_0_, bf16[256,1024]{1,0:T(8,128)(2,1)} %get-tuple-element.30.refs_1_, bf16[256,1024]{1,0:T(8,128)(2,1)} %get-tuple-element.31.refs_2_, bf16[256,1024]{1,0:T(8,128)(2,1)} %get-tuple-element.32.rows_ref.refs_3_, ...), custom_call_target="tpu_custom_call" | custom-call | flops 2147483648 | bytes 4194304 | tf_op jit(solution)/shard_map/weights/pallas_call | solution.py:271
  64.6 7.5 %all-to-all-done.1 = bf16[128,8,512]{2,1,0:T(8,128)(2,1)S(1)} async-done(((bf16[128,8,512]{2,1,0:T(8,128)(2,1)}), bf16[128,8,512]{2,1,0:T(8,128)(2,1)S(1)}, u32[]{:S(2)}, u32[]{:S(2)}) %all-to-all-start.1) | async-done | bytes 1048608 | tf_op jit(solution)/shard_map/all_to_all | solution.py:319
  72.1 1.0 %unpack.1 = bf16[128,512]{1,0:T(8,128)(2,1)} custom-call(s32[1,128]{1,0:T(1,128)S(1)} %get-tuple-element.23.slots_ref, bf16[32,4,8,512]{3,2,1,0:T(8,128)(2,1)S(1)} %bitcast.23), custom_call_target="tpu_custom_call" | custom-call | tf_op jit(solution)/shard_map/unpack/pallas_call | solution.py:84
  (1 shorter events, 0.0 us)
Async XLA Ops:
  0.6 33.7 %copy-start.1 = (bf16[1,1024,512]{2,1,0:T(8,128)(2,1)S(1)}, bf16[1,1024,512]{2,1,0:T(8,128)(2,1)}, u32[]{:S(2)}) copy-start(bf16[1,1024,512]{2,1,0:T(8,128)(2,1)} %param.9) | copy-start | bytes 3145732
  0.6 33.7 %copy-start = (bf16[1,512,1024]{2,1,0:T(8,128)(2,1)S(1)}, bf16[1,512,1024]{2,1,0:T(8,128)(2,1)}, u32[]{:S(2)}) copy-start(bf16[1,512,1024]{2,1,0:T(8,128)(2,1)} %param.8) | copy-start | bytes 3145732
  22.9 8.1 %collective-permute-start.2 = (bf16[128,1024]{1,0:T(8,128)(2,1)S(1)}, bf16[128,1024]{1,0:T(8,128)(2,1)S(1)}, u32[]{:S(2)}, u32[]{:S(2)}) collective-permute-start(bf16[128,1024]{1,0:T(8,128)(2,1)S(1)} %get-tuple-element.43.refs_1_), channel_id=1, source_target_pairs={{0,3},{1,0},{2,1},{3,2},{4,7},{5,4},{6,5},{7,6},{8,11},{9,8},{10,9... | collective-permute-start | bytes 786440 | tf_op jit(solution)/shard_map/ppermute | solution.py:307
  25.7 8.7 %collective-permute-start = (bf16[128,1024]{1,0:T(8,128)(2,1)S(1)}, bf16[128,1024]{1,0:T(8,128)(2,1)}, u32[]{:S(2)}, u32[]{:S(2)}) collective-permute-start(bf16[128,1024]{1,0:T(8,128)(2,1)S(1)} %get-tuple-element.44.refs_0_), channel_id=1, source_target_pairs={{0,1},{1,2},{2,3},{3,0},{4,5},{5,6},{6,7},{7,4},{8,9},{9,10},{10,1... | collective-permute-start | bytes 786440 | tf_op jit(solution)/shard_map/ppermute | solution.py:307
  25.7 14.1 %collective-permute-start.5 = (bf16[128,1024]{1,0:T(8,128)(2,1)S(1)}, bf16[128,1024]{1,0:T(8,128)(2,1)}, u32[]{:S(2)}, u32[]{:S(2)}) collective-permute-start(bf16[128,1024]{1,0:T(8,128)(2,1)S(1)} %get-tuple-element.43.refs_1_), channel_id=1, source_target_pairs={{0,1},{1,2},{2,3},{3,0},{4,5},{5,6},{6,7},{7,4},{8,9},{9,10},{10,1... | collective-permute-start | bytes 786440 | tf_op jit(solution)/shard_map/ppermute | solution.py:307
  25.7 14.1 %collective-permute-start.4 = (bf16[128,1024]{1,0:T(8,128)(2,1)S(1)}, bf16[128,1024]{1,0:T(8,128)(2,1)}, u32[]{:S(2)}, u32[]{:S(2)}) collective-permute-start(bf16[128,1024]{1,0:T(8,128)(2,1)S(1)} %get-tuple-element.44.refs_0_), channel_id=1, source_target_pairs={{0,3},{1,0},{2,1},{3,2},{4,7},{5,4},{6,5},{7,6},{8,11},{9,8},{10,9... | collective-permute-start | bytes 786440 | tf_op jit(solution)/shard_map/ppermute | solution.py:307
  30.9 12.0 %collective-permute-start.3 = (bf16[128,1024]{1,0:T(8,128)(2,1)S(1)}, bf16[128,1024]{1,0:T(8,128)(2,1)S(1)}, u32[]{:S(2)}, u32[]{:S(2)}) collective-permute-start(bf16[128,1024]{1,0:T(8,128)(2,1)S(1)} %collective-permute-done.2.refs_1_), channel_id=1, source_target_pairs={{0,3},{1,0},{2,1},{3,2},{4,7},{5,4},{6,5},{7,6},{8,11},{9,8},{10,9... | collective-permute-start | bytes 786440 | tf_op jit(solution)/shard_map/ppermute | solution.py:307
  34.4 11.0 %collective-permute-start.1 = (bf16[128,1024]{1,0:T(8,128)(2,1)}, bf16[128,1024]{1,0:T(8,128)(2,1)S(1)}, u32[]{:S(2)}, u32[]{:S(2)}) collective-permute-start(bf16[128,1024]{1,0:T(8,128)(2,1)} %collective-permute-done.refs_0_), channel_id=1, source_target_pairs={{0,1},{1,2},{2,3},{3,0},{4,5},{5,6},{6,7},{7,4},{8,9},{9,10},{10,1... | collective-permute-start | bytes 786440 | tf_op jit(solution)/shard_map/ppermute | solution.py:307
  47.5 24.6 %all-to-all-start.1 = ((bf16[128,8,512]{2,1,0:T(8,128)(2,1)}), bf16[128,8,512]{2,1,0:T(8,128)(2,1)S(1)}, u32[]{:S(2)}, u32[]{:S(2)}) async-start(bf16[128,8,512]{2,1,0:T(8,128)(2,1)} %bitcast.25), calls=%async_computation.1 | async-start | bytes 2097152 | tf_op jit(solution)/shard_map/all_to_all | solution.py:319
where the time goes:
time: 73.4 us; the launch traced here: 73 us
  Pallas kernels  24.6 us (34%)
  blocking collectives  20.7 us (28%)
  starting transfers between devices  14.2 us (19%)
  waiting for transfers between devices  12.8 us (17%)
    all_to_all x1, blocking collectives, steps(): lax.all_to_all(packed.reshape(experts, capacity, 2 * width), 'expert', sp...  20.7 us
    ppermute x6, starting transfers between devices, send(): return lax.ppermute(rows, 'replica', way)  8.91 us
    pallas_call x3, Pallas kernels, group(): pl.pallas_call(functools.partial(group_kernel, len(pieces)), out_shape=(p...  8.15 us
    all_to_all x1, waiting for transfers between devices, steps(): lax.all_to_all(sending.reshape(experts * replicas, capacity, width), ('ex...  7.49 us
    pallas_call x1, Pallas kernels, weight_grads(): pl.pallas_call(functools.partial(weights_kernel, len(pieces), len(acts)),...  7.38 us
    ppermute x6, waiting for transfers between devices, send(): return lax.ppermute(rows, 'replica', way)  5.32 us
    all_to_all x1, starting transfers between devices, steps(): lax.all_to_all(sending.reshape(experts * replicas, capacity, width), ('ex...  5.28 us
    pallas_call x1, Pallas kernels, again(): pl.pallas_call(again_kernel, out_shape=(out, out), grid=(hidden // tile,)...  4.44 us
  transfers between devices with their start and end apart: 7, of which 4 were waited for; matrix products, arithmetic and copies ran while one was open for 0% of the time, Pallas kernels for 27%

commit v1 on v0

--- a/solution.py
+++ b/solution.py
@@ -141,16 +141,15 @@
         copy.wait()
 
 
-def last_kernel(count, where_ref, *refs):
+def last_kernel(count, cut, where_ref, *refs):
     win_ref, wout_ref, own_ref, near_ref, late_ref, out_hbm, rows_hbm, part, sems, rows_sems = refs[count:]
     sources, replicas = out_hbm.shape[:2]
-    cut = sources // 2
     at = [lax.rem(where_ref[0] + k, replicas) for k in range(replicas)]
     copies = []
 
     def put(ref, low, high):
-        for first, replica in ((0, low), (cut, high)):
-            rows = pl.ds(first, cut)
+        for first, some, replica in ((0, cut, low), (cut, sources - cut, high)):
+            rows = pl.ds(first, some)
             copies.append(pltpu.make_async_copy(ref.at[rows], out_hbm.at[rows, replica], sems.at[len(copies)]))
             copies[-1].start()
 
@@ -200,7 +199,7 @@
     width, hidden = win.shape
     sources, capacity = own.shape[:2]
     return pl.pallas_call(
-        functools.partial(last_kernel, len(pieces)),
+        functools.partial(last_kernel, len(pieces), pieces[0].shape[0] // capacity),
         out_shape=(
             pltpu.HBM((sources, replicas, capacity, width), BF16),
             pltpu.HBM((rows, 2 * width), BF16),
@@ -300,7 +299,7 @@
     ).reshape(experts * capacity, 2 * width)
     up = [(i, (i + 1) % replicas) for i in range(replicas)]
     down = [(i, (i - 1) % replicas) for i in range(replicas)]
-    half = experts * capacity // 2
+    half = 9 * experts * capacity // 16
     low, high = own[:half], own[half:]
 
     def send(rows, way):

time: 73.4 us -> 72.3 us (0.985)
  starting transfers between devices: 14.2 us -> 12.7 us
    ppermute x6, starting transfers between devices: 8.91 us -> 7.03 us  [send(): return lax.ppermute(rows, 'replica', way)]
  transfers between devices with their start and end apart: 7 -> 7, of which waited for: 4 -> 3; matrix products, arithmetic and copies ran while one was open for 0% -> 0% of each run, Pallas kernels for 27% -> 28%
where the time goes in v1:
time: 72.3 us; the launch traced here: 71.9 us
  Pallas kernels  24.6 us (34%)
  blocking collectives  20.7 us (29%)
  waiting for transfers between devices  13.2 us (18%)
  starting transfers between devices  12.7 us (18%)
  between operations  0.73 us (1%)
    all_to_all x1, blocking collectives, steps(): lax.all_to_all(packed.reshape(experts, capacity, 2 * width), 'expert', sp...  20.7 us
    pallas_call x3, Pallas kernels, group(): pl.pallas_call(functools.partial(group_kernel, len(pieces)), out_shape=(p...  8.14 us
    all_to_all x1, waiting for transfers between devices, steps(): lax.all_to_all(sending.reshape(experts * replicas, capacity, width), ('ex...  7.62 us
    pallas_call x1, Pallas kernels, weight_grads(): pl.pallas_call(functools.partial(weights_kernel, len(pieces), len(acts)),...  7.38 us
    ppermute x6, starting transfers between devices, send(): return lax.ppermute(rows, 'replica', way)  7.03 us
    all_to_all x1, starting transfers between devices, steps(): lax.all_to_all(sending.reshape(experts * replicas, capacity, width), ('ex...  5.65 us
    ppermute x6, waiting for transfers between devices, send(): return lax.ppermute(rows, 'replica', way)  5.56 us
    pallas_call x1, Pallas kernels, again(): pl.pallas_call(again_kernel, out_shape=(out, out), grid=(hidden // tile,)...  4.44 us
  transfers between devices with their start and end apart: 7, of which 3 were waited for; matrix products, arithmetic and copies ran while one was open for 0% of the time, Pallas kernels for 28%

profile of v1, /device:TPU:1, one launch (start us, length us, event | category | flops | bytes accessed | tf_op | source)
XLA Modules:
  0.0 71.9 jit_solution(7192392756379189371)
XLA Ops:
  0.6 0.0 copy-start.1
  0.6 0.0 copy-start
  0.7 1.5 %pack.1 = (bf16[256,1024]{1,0:T(8,128)(2,1)S(1)}, s32[1,128]{1,0:T(1,128)S(1)}) custom-call(s32[1,128]{1,0:T(1,128)} %bitcast.26, bf16[128,512]{1,0:T(8,128)(2,1)} %rows_hbm.1, bf16[128,512]{1,0:T(8,128)(2,1)} %grad_hbm.1), custom_call_target="tpu_custom_call" | custom-call | tf_op jit(solution)/shard_map/pack/pallas_call | solution.py:56
  2.2 20.7 %all_to_all.10 = bf16[32,8,1024]{2,1,0:T(8,128)(2,1)S(1)} all-to-all(bf16[32,8,1024]{2,1,0:T(8,128)(2,1)S(1)} %bitcast.24), channel_id=1, replica_groups=mesh['expert'=32,'replica'=4] {'expert'}, dimensions={0} | all-to-all | bytes 1048576 | tf_op jit(solution)/shard_map/all_to_all | solution.py:297
  22.9 1.4 %collective-permute-start = (bf16[144,1024]{1,0:T(8,128)(2,1)S(1)}, bf16[144,1024]{1,0:T(8,128)(2,1)S(1)}, u32[]{:S(2)}, u32[]{:S(2)}) collective-permute-start(bf16[144,1024]{1,0:T(8,128)(2,1)S(1)} %slice_bitcast_fusion.refs_0_), channel_id=1, source_target_pairs={{0,1},{1,2},{2,3},{3,0},{4,5},{5,6},{6,7},{7,4},{8,9},{9,10},{10,1... | collective-permute-start | bytes 884744 | tf_op jit(solution)/shard_map/ppermute | solution.py:306
  24.3 1.5 %collective-permute-start.2 = (bf16[112,1024]{1,0:T(8,128)(2,1)S(1)}, bf16[112,1024]{1,0:T(8,128)(2,1)}, u32[]{:S(2)}, u32[]{:S(2)}) collective-permute-start(bf16[112,1024]{1,0:T(8,128)(2,1)S(1)} %slice_bitcast_fusion.1.refs_1_), channel_id=1, source_target_pairs={{0,3},{1,0},{2,1},{3,2},{4,7},{5,4},{6,5},{7,6},{8,11},{9,8},{10,9... | collective-permute-start | bytes 688136 | tf_op jit(solution)/shard_map/ppermute | solution.py:306
  25.8 1.4 %collective-permute-start.4 = (bf16[144,1024]{1,0:T(8,128)(2,1)S(1)}, bf16[144,1024]{1,0:T(8,128)(2,1)}, u32[]{:S(2)}, u32[]{:S(2)}) collective-permute-start(bf16[144,1024]{1,0:T(8,128)(2,1)S(1)} %slice_bitcast_fusion.refs_0_), channel_id=1, source_target_pairs={{0,3},{1,0},{2,1},{3,2},{4,7},{5,4},{6,5},{7,6},{8,11},{9,8},{10,9... | collective-permute-start | bytes 884744 | tf_op jit(solution)/shard_map/ppermute | solution.py:306
  27.2 0.0 collective-permute-start.5
  27.2 5.2 %collective-permute-done.refs_0_ = bf16[144,1024]{1,0:T(8,128)(2,1)S(1)} collective-permute-done((bf16[144,1024]{1,0:T(8,128)(2,1)S(1)}, bf16[144,1024]{1,0:T(8,128)(2,1)S(1)}, u32[]{:S(2)}, u32[]{:S(2)}) %collective-permute-start) | collective-permute-done | bytes 294944 | tf_op jit(solution)/shard_map/ppermute | solution.py:306
  32.4 0.1 collective-permute-start.1
  32.5 0.0 collective-permute-done.2.refs_1_
  32.5 2.6 %collective-permute-start.3 = (bf16[112,1024]{1,0:T(8,128)(2,1)}, bf16[112,1024]{1,0:T(8,128)(2,1)S(1)}, u32[]{:S(2)}, u32[]{:S(2)}) collective-permute-start(bf16[112,1024]{1,0:T(8,128)(2,1)} %collective-permute-done.2.refs_1_), channel_id=1, source_target_pairs={{0,3},{1,0},{2,1},{3,2},{4,7},{5,4},{6,5},{7,6},{8,11},{9,8},{10,9... | collective-permute-start | bytes 688136 | tf_op jit(solution)/shard_map/ppermute | solution.py:306
  35.1 0.0 copy-done.1
  35.1 0.0 copy-done
  35.1 2.1 %group.3 = (bf16[256,1024]{1,0:T(8,128)(2,1)}, bf16[256,1024]{1,0:T(8,128)(2,1)}, bf16[256,1024]{1,0:T(8,128)(2,1)}, bf16[32,8,512]{2,1,0:T(8,128)(2,1)S(1)}) custom-call(bf16[144,1024]{1,0:T(8,128)(2,1)S(1)} %slice_bitcast_fusion.refs_0_, bf16[112,1024]{1,0:T(8,128)(2,1)S(1)} %slice_bitcast_fusion.1.refs_1_, bf16[512,1024]{1,0:T(8,128)(2,1)S(1)} %bitcast.14, ...), custom_call_target="tpu_custom_call" | custom-call | flops 805306368 | bytes 2097152 | tf_op jit(solution)/shard_map/group/pallas_call | solution.py:175
  37.2 3.0 %group.4 = (bf16[256,1024]{1,0:T(8,128)(2,1)}, bf16[256,1024]{1,0:T(8,128)(2,1)}, bf16[256,1024]{1,0:T(8,128)(2,1)}, bf16[32,8,512]{2,1,0:T(8,128)(2,1)S(1)}) custom-call(bf16[144,1024]{1,0:T(8,128)(2,1)S(1)} %collective-permute-done.refs_0_, bf16[112,1024]{1,0:T(8,128)(2,1)} %collective-permute-done.2.refs_1_, bf16[512,1024]{1,0:T(8,128)(2,1)S(1)} %bitcast.15, ...), custom_call_target="tpu_custom_call" | custom-call | flops 805306368 | bytes 2097152 | tf_op jit(solution)/shard_map/group/pallas_call | solution.py:175
  40.2 0.0 collective-permute-done.5.refs_1_
  40.2 0.0 collective-permute-done.4.refs_0_
  40.2 3.1 %group.5 = (bf16[256,1024]{1,0:T(8,128)(2,1)}, bf16[256,1024]{1,0:T(8,128)(2,1)}, bf16[256,1024]{1,0:T(8,128)(2,1)}, bf16[32,8,512]{2,1,0:T(8,128)(2,1)S(1)}) custom-call(bf16[144,1024]{1,0:T(8,128)(2,1)} %collective-permute-done.4.refs_0_, bf16[112,1024]{1,0:T(8,128)(2,1)} %collective-permute-done.5.refs_1_, bf16[512,1024]{1,0:T(8,128)(2,1)S(1)} %bitcast.16, ...), custom_call_target="tpu_custom_call" | custom-call | flops 805306368 | bytes 2097152 | tf_op jit(solution)/shard_map/group/pallas_call | solution.py:175
  43.3 0.0 collective-permute-done.3.refs_1_
  43.3 0.4 collective-permute-done.1.refs_0_
  43.7 2.2 %last_group.1 = (bf16[32,4,8,512]{3,2,1,0:T(8,128)(2,1)}, bf16[256,1024]{1,0:T(8,128)(2,1)}) custom-call(s32[1]{0:T(128)} %bitcast.1.where_ref, bf16[144,1024]{1,0:T(8,128)(2,1)S(1)} %collective-permute-done.1.refs_0_, bf16[112,1024]{1,0:T(8,128)(2,1)S(1)} %collective-permute-done.3.refs_1_, bf16[512,1024]{1,0:T(8,128)(2,1)S(1)} %bitcast.17, ...), custom_call_target="tpu_custom_call" | custom-call | flops 805306368 | bytes 2097152 | tf_op jit(solution)/shard_map/last_group/pallas_call | solution.py:201
  45.8 5.7 %all-to-all-start.1 = ((bf16[128,8,512]{2,1,0:T(8,128)(2,1)}), bf16[128,8,512]{2,1,0:T(8,128)(2,1)S(1)}, u32[]{:S(2)}, u32[]{:S(2)}) async-start(bf16[128,8,512]{2,1,0:T(8,128)(2,1)} %bitcast.25), calls=%async_computation.1 | async-start | bytes 2097152 | tf_op jit(solution)/shard_map/all_to_all | solution.py:318
  51.5 4.4 %again.1 = (bf16[256,1024]{1,0:T(8,128)(2,1)}, bf16[256,1024]{1,0:T(8,128)(2,1)}) custom-call(bf16[256,1024]{1,0:T(8,128)(2,1)} %get-tuple-element.32.rows_ref.refs_3_, bf16[512,1024]{1,0:T(8,128)(2,1)} %bitcast.13, bf16[1024,512]{1,0:T(8,128)(2,1)} %bitcast.18), custom_call_target="tpu_custom_call" | custom-call | flops 536870912 | bytes 2097152 | tf_op jit(solution)/shard_map/again/pallas_call | solution.py:230
  56.0 7.4 %weights.1 = (f32[512,1024]{1,0:T(8,128)}, f32[1024,512]{1,0:T(8,128)}) custom-call(bf16[256,1024]{1,0:T(8,128)(2,1)} %get-tuple-element.29.refs_0_, bf16[256,1024]{1,0:T(8,128)(2,1)} %get-tuple-element.30.refs_1_, bf16[256,1024]{1,0:T(8,128)(2,1)} %get-tuple-element.31.refs_2_, bf16[256,1024]{1,0:T(8,128)(2,1)} %get-tuple-element.32.rows_ref.refs_3_, ...), custom_call_target="tpu_custom_call" | custom-call | flops 2147483648 | bytes 4194304 | tf_op jit(solution)/shard_map/weights/pallas_call | solution.py:270
  63.3 7.6 %all-to-all-done.1 = bf16[128,8,512]{2,1,0:T(8,128)(2,1)S(1)} async-done(((bf16[128,8,512]{2,1,0:T(8,128)(2,1)}), bf16[128,8,512]{2,1,0:T(8,128)(2,1)S(1)}, u32[]{:S(2)}, u32[]{:S(2)}) %all-to-all-start.1) | async-done | bytes 1048608 | tf_op jit(solution)/shard_map/all_to_all | solution.py:318
  71.0 1.0 %unpack.1 = bf16[128,512]{1,0:T(8,128)(2,1)} custom-call(s32[1,128]{1,0:T(1,128)S(1)} %get-tuple-element.23.slots_ref, bf16[32,4,8,512]{3,2,1,0:T(8,128)(2,1)S(1)} %bitcast.23), custom_call_target="tpu_custom_call" | custom-call | tf_op jit(solution)/shard_map/unpack/pallas_call | solution.py:84
  (2 shorter events, 0.0 us)
Async XLA Ops:
  0.6 34.5 %copy-start.1 = (bf16[1,1024,512]{2,1,0:T(8,128)(2,1)S(1)}, bf16[1,1024,512]{2,1,0:T(8,128)(2,1)}, u32[]{:S(2)}) copy-start(bf16[1,1024,512]{2,1,0:T(8,128)(2,1)} %param.9) | copy-start | bytes 3145732
  0.6 34.5 %copy-start = (bf16[1,512,1024]{2,1,0:T(8,128)(2,1)S(1)}, bf16[1,512,1024]{2,1,0:T(8,128)(2,1)}, u32[]{:S(2)}) copy-start(bf16[1,512,1024]{2,1,0:T(8,128)(2,1)} %param.8) | copy-start | bytes 3145732
  22.9 9.6 %collective-permute-start = (bf16[144,1024]{1,0:T(8,128)(2,1)S(1)}, bf16[144,1024]{1,0:T(8,128)(2,1)S(1)}, u32[]{:S(2)}, u32[]{:S(2)}) collective-permute-start(bf16[144,1024]{1,0:T(8,128)(2,1)S(1)} %slice_bitcast_fusion.refs_0_), channel_id=1, source_target_pairs={{0,1},{1,2},{2,3},{3,0},{4,5},{5,6},{6,7},{7,4},{8,9},{9,10},{10,1... | collective-permute-start | bytes 884744 | tf_op jit(solution)/shard_map/ppermute | solution.py:306
  24.3 8.3 %collective-permute-start.2 = (bf16[112,1024]{1,0:T(8,128)(2,1)S(1)}, bf16[112,1024]{1,0:T(8,128)(2,1)}, u32[]{:S(2)}, u32[]{:S(2)}) collective-permute-start(bf16[112,1024]{1,0:T(8,128)(2,1)S(1)} %slice_bitcast_fusion.1.refs_1_), channel_id=1, source_target_pairs={{0,3},{1,0},{2,1},{3,2},{4,7},{5,4},{6,5},{7,6},{8,11},{9,8},{10,9... | collective-permute-start | bytes 688136 | tf_op jit(solution)/shard_map/ppermute | solution.py:306
  25.8 14.4 %collective-permute-start.4 = (bf16[144,1024]{1,0:T(8,128)(2,1)S(1)}, bf16[144,1024]{1,0:T(8,128)(2,1)}, u32[]{:S(2)}, u32[]{:S(2)}) collective-permute-start(bf16[144,1024]{1,0:T(8,128)(2,1)S(1)} %slice_bitcast_fusion.refs_0_), channel_id=1, source_target_pairs={{0,3},{1,0},{2,1},{3,2},{4,7},{5,4},{6,5},{7,6},{8,11},{9,8},{10,9... | collective-permute-start | bytes 884744 | tf_op jit(solution)/shard_map/ppermute | solution.py:306
  27.2 13.0 %collective-permute-start.5 = (bf16[112,1024]{1,0:T(8,128)(2,1)S(1)}, bf16[112,1024]{1,0:T(8,128)(2,1)}, u32[]{:S(2)}, u32[]{:S(2)}) collective-permute-start(bf16[112,1024]{1,0:T(8,128)(2,1)S(1)} %slice_bitcast_fusion.1.refs_1_), channel_id=1, source_target_pairs={{0,1},{1,2},{2,3},{3,0},{4,5},{5,6},{6,7},{7,4},{8,9},{9,10},{10,1... | collective-permute-start | bytes 688136 | tf_op jit(solution)/shard_map/ppermute | solution.py:306
  32.4 11.2 %collective-permute-start.1 = (bf16[144,1024]{1,0:T(8,128)(2,1)S(1)}, bf16[144,1024]{1,0:T(8,128)(2,1)S(1)}, u32[]{:S(2)}, u32[]{:S(2)}) collective-permute-start(bf16[144,1024]{1,0:T(8,128)(2,1)S(1)} %collective-permute-done.refs_0_), channel_id=1, source_target_pairs={{0,1},{1,2},{2,3},{3,0},{4,5},{5,6},{6,7},{7,4},{8,9},{9,10},{10,1... | collective-permute-start | bytes 884744 | tf_op jit(solution)/shard_map/ppermute | solution.py:306
  32.5 10.8 %collective-permute-start.3 = (bf16[112,1024]{1,0:T(8,128)(2,1)}, bf16[112,1024]{1,0:T(8,128)(2,1)S(1)}, u32[]{:S(2)}, u32[]{:S(2)}) collective-permute-start(bf16[112,1024]{1,0:T(8,128)(2,1)} %collective-permute-done.2.refs_1_), channel_id=1, source_target_pairs={{0,3},{1,0},{2,1},{3,2},{4,7},{5,4},{6,5},{7,6},{8,11},{9,8},{10,9... | collective-permute-start | bytes 688136 | tf_op jit(solution)/shard_map/ppermute | solution.py:306
  45.8 25.1 %all-to-all-start.1 = ((bf16[128,8,512]{2,1,0:T(8,128)(2,1)}), bf16[128,8,512]{2,1,0:T(8,128)(2,1)S(1)}, u32[]{:S(2)}, u32[]{:S(2)}) async-start(bf16[128,8,512]{2,1,0:T(8,128)(2,1)} %bitcast.25), calls=%async_computation.1 | async-start | bytes 2097152 | tf_op jit(solution)/shard_map/all_to_all | solution.py:318
